TPU v7x, 256 devices: a whole 4x4x8 slice. The times are simulated.
256 devices in a mesh: space: 16 (over x, z_hi), tm: 16 (over y, z_lo, core).
Axes of the slice: x: 4, y: 4, z: 8 (z_hi: 4, z_lo: 2; z = z_hi * 2 + z_lo), core: 2. Of those that a mesh axis runs over, the one named last changes fastest.
Arguments:
- latent: float32 [24, 1024, 2048], P(None, 'space', 'tm'), may hold values from -1.8 to 1.8
- events: int32 [24, 1024, 2048], P(None, 'space', 'tm'), may hold values from 0 to 7
- log_base: float32 [24, 1024, 2048], P(None, 'space', 'tm'), may hold values from -1.5 to 0.5
- innovation: float32 [24, 1024, 2048], P(None, 'space', 'tm'), may hold values from -6 to 6
- kappa_sq: float32 [24, 1024], replicated, may hold values from 0.3 to 3
- chol_factor: float32 [2048, 2048], P(None, 'tm'), as said below
- step_size: float32 [1], replicated, may hold values from 0.02 to 0.08
Outputs:
- gradient: float32 [24, 1024, 2048], P(None, 'space', 'tm')
- proposal: float32 [24, 1024, 2048], P(None, 'space', 'tm')
Inputs may be any that keep to these rules, and one draw needn't show every extreme that they name: chol_factor is lower triangular with a positive diagonal.
All inputs are finite; a program needn't handle non-finite values.
Results may differ from a plain program's by a relative error of at most 0.000067.
Values sent between devices are 32-bit elements; how exact they have to be, the bound alone decides.
A program may use at most 64 MiB of HBM per device.

v0:
```python
import jax
import jax.numpy as jnp
from jax import lax
from jax.sharding import PartitionSpec as P


def halo(block, width):
    count = lax.axis_size("space")
    forward = [(i, i + 1) for i in range(count - 1)]
    backward = [(target, source) for source, target in forward]
    cols = block.shape[1]
    low = lax.ppermute(lax.slice_in_dim(block, cols - width, None, axis=1), "space", forward)
    high = lax.ppermute(lax.slice_in_dim(block, 0, width, axis=1), "space", backward)
    return jnp.concatenate([low, block, high], axis=1)


def operate(extended, kappa_cols):
    centre = extended[:, 1:-1]
    row_padded = jnp.pad(centre, ((1, 1), (0, 0), (0, 0)))
    beside = row_padded[2:] + row_padded[:-2]
    beside = beside + extended[:, 2:] + extended[:, :-2]
    return (kappa_cols[:, :, None] + 4.0) * centre - beside


def gather_factor(chol_cols):
    n = lax.axis_size("tm")
    T, B = chol_cols.shape
    H = (n + 1) * B // 2
    tail = T - H
    j = lax.axis_index("tm")
    pairs = [(i, n - 1 - i) for i in range(n // 2)]
    sent = lax.ppermute(chol_cols[T - tail :], "tm", pairs)
    own_low = lax.dynamic_slice_in_dim(chol_cols, j * B, H, axis=0)
    partner = n - 1 - j
    length = (n - partner) * B - H
    shifted = lax.dynamic_slice_in_dim(
        jnp.concatenate([sent, jnp.zeros((H, B), sent.dtype)], axis=0), tail - length, H, axis=0
    )
    own_tail = chol_cols[T - H :]
    rows = lax.broadcasted_iota(jnp.int32, (H, B), 0)
    own_high = jnp.where(rows < length, shifted, own_tail)
    piece = jnp.where(j < n // 2, own_low, own_high)
    gathered = lax.all_gather(piece, "tm", axis=0, tiled=False)
    blocks = []
    for c in range(n):
        if c < n // 2:
            p = n - 1 - c
            length_c = (n - c) * B - H
            nonzero = jnp.concatenate([gathered[c], gathered[p, :length_c]], axis=0)
        else:
            p = n - 1 - c
            length_p = (n - p) * B - H
            nonzero = gathered[c, length_p:]
        blocks.append(jnp.concatenate([jnp.zeros((c * B, B), nonzero.dtype), nonzero], axis=0))
    return jnp.concatenate(blocks, axis=1)


def local(latent, events, log_base, innovation, kappa_sq, chol_factor, step_size):
    row_count, col_count, time_count = latent.shape
    space_count = lax.axis_size("space")
    col_index = lax.axis_index("space")
    padded_kappa = jnp.pad(kappa_sq, ((0, 0), (1, 1)))
    kappa_wide = lax.dynamic_slice(
        padded_kappa, (jnp.int32(0), col_index * col_count), (row_count, col_count + 2)
    )
    full = gather_factor(chol_factor)
    extended = halo(latent, 2)
    first_pass = operate(extended, kappa_wide)
    cols = lax.broadcasted_iota(jnp.int32, (1, col_count + 2, 1), 1)
    outside = (cols == 0) & (col_index == 0) | (cols == col_count + 1) & (
        col_index == space_count - 1
    )
    first_pass = jnp.where(outside, 0.0, first_pass)
    spatial = operate(first_pass, kappa_wide[:, 1:-1])
    cell_count = row_count * col_count
    flattened = spatial.reshape(cell_count, time_count)
    by_cell = lax.all_to_all(flattened, "tm", 0, 1, tiled=True)
    projected = jnp.dot(
        by_cell, full, precision=lax.Precision.HIGHEST, preferred_element_type=jnp.float32
    )
    prior_cells = lax.dot_general(
        projected,
        full,
        (((1,), (1,)), ((), ())),
        precision=lax.Precision.HIGHEST,
        preferred_element_type=jnp.float32,
    )
    prior = lax.all_to_all(prior_cells, "tm", 1, 0, tiled=True)
    prior_term = prior.reshape(row_count, col_count, time_count)
    gradient = events.astype(jnp.float32) - jnp.exp(log_base + latent) - prior_term
    proposal = latent + step_size[0] * gradient + jnp.sqrt(2.0 * step_size[0]) * innovation
    return (gradient, proposal)


def solution(mesh):
    in_specs = (
        P(None, "space", "tm"),
        P(None, "space", "tm"),
        P(None, "space", "tm"),
        P(None, "space", "tm"),
        P(),
        P(None, "tm"),
        P(),
    )
    out_specs = (P(None, "space", "tm"), P(None, "space", "tm"))
    return jax.shard_map(local, mesh=mesh, in_specs=in_specs, out_specs=out_specs, check_vma=False)
```

profile of v0, /device:TPU:1, one launch (start us, length us, event | category | flops | bytes accessed | tf_op | source)
XLA Modules:
  0.0 197.4 jit_solution(2388541145353253370)
XLA Ops:
  8.3 7.4 %collective-permute-start.2 = (f32[960,128]{1,0:T(8,128)S(1)}, f32[960,128]{1,0:T(8,128)S(1)}, u32[]{:S(2)}, u32[]{:S(2)}) collective-permute-start(f32[960,128]{1,0:T(8,128)S(1)} %slice.126), channel_id=1, source_target_pairs={{0,15},{1,14},{2,13},{3,12},{4,11},{5,10},{6,9},{7,8},{16,31},{17,... | collective-permute-start | bytes 1474568 | tf_op jit(solution)/shard_map/ppermute | solution.py:32
  15.7 11.0 %collective-permute-done.2 = f32[960,128]{1,0:T(8,128)S(1)} collective-permute-done((f32[960,128]{1,0:T(8,128)S(1)}, f32[960,128]{1,0:T(8,128)S(1)}, u32[]{:S(2)}, u32[]{:S(2)}) %collective-permute-start.2) | collective-permute-done | bytes 491552 | tf_op jit(solution)/shard_map/ppermute | solution.py:32
  26.7 2.3 %fusion.13 = f32[1088,128]{1,0:T(8,128)} fusion(s32[]{:T(128)S(6)} %select_n.29, f32[960,128]{1,0:T(8,128)S(1)} %collective-permute-done.2, f32[2048,128]{1,0:T(8,128)} %param.12, s32[]{:T(128)S(6)} %select_n.28, pred[1088]{0:T(1024)(128)(4,1)S(1)} %iota_compare_fusion, pred[]{:T(512)S(6)} %lt.20), kind=kLoop, calls=%fused_computation.40 | loop fusion | flops 278528 | bytes 2163785 | tf_op jit(solution)/shard_map/jit(_where)/select_n | solution.py:42
  29.9 4.9 %collective-permute-start = (f32[24,2,128]{2,1,0:T(2,128)S(1)}, f32[24,2,128]{2,1,0:T(2,128)S(1)}, u32[]{:S(2)}, u32[]{:S(2)}) collective-permute-start(f32[24,2,128]{2,1,0:T(2,128)S(1)} %get-tuple-element.12), channel_id=1, source_target_pairs={{0,16},{16,32},{32,48},{48,64},{64,80},{80,96},{96,112},{112,128},... | collective-permute-start | bytes 73736 | tf_op jit(solution)/shard_map/ppermute | solution.py:12
  34.8 1.3 collective-permute-start.1
  38.0 3.3 %collective-permute-done.1 = f32[24,2,128]{2,1,0:T(2,128)S(1)} collective-permute-done((f32[24,2,128]{2,1,0:T(2,128)S(1)}, f32[24,2,128]{2,1,0:T(2,128)S(1)}, u32[]{:S(2)}, u32[]{:S(2)}) %collective-permute-start.1) | collective-permute-done | bytes 24608 | tf_op jit(solution)/shard_map/ppermute | solution.py:13
  41.3 1.2 pad_maximum_fusion
  42.5 1.7 fusion.4
  44.3 1.2 fusion.8
  45.5 7.7 %all-to-all-start = ((f32[16,96,128]{2,1,0:T(8,128)}), f32[16,96,128]{2,1,0:T(8,128)S(1)}, u32[]{:S(2)}, u32[]{:S(2)}) async-start(f32[16,96,128]{2,1,0:T(8,128)} %bitcast), calls=%async_computation | async-start | bytes 1572864 | tf_op jit(solution)/shard_map/all_to_all | solution.py:77
  53.2 44.7 %all-gather.3.cloned.1.call-done = f32[17408,128]{1,0:T(8,128)} async-done(((f32[1088,128]{1,0:T(8,128)}), f32[17408,128]{1,0:T(8,128)}) %all-gather.3.cloned.1.call-update) | async-done | bytes 8912912 | tf_op jit(solution)/shard_map/all_gather | solution.py:43
  111.5 1.1 slice_bitcast_fusion
  112.6 2.6 %fusion.16 = (f32[1088,128]{1,0:T(8,128)S(1)}, f32[1088,128]{1,0:T(8,128)S(1)}, f32[1088,128]{1,0:T(8,128)S(1)}, f32[1088,128]{1,0:T(8,128)S(1)}, f32[1088,128]{...) fusion(f32[17408,128]{1,0:T(8,128)} %all-gather.3.cloned.1.call-done), kind=kLoop, calls=%fused_computation.63 | loop fusion | bytes 8912896 | tf_op jit(solution)/shard_map/slice | solution.py:49
  115.1 1.1 maximum_dynamic-update-slice_fusion.7
  116.2 1.4 maximum_dynamic-update-slice_fusion.6
  117.6 1.4 maximum_dynamic-update-slice_fusion.5
  119.0 1.4 maximum_dynamic-update-slice_fusion.4
  120.4 1.4 maximum_dynamic-update-slice_fusion.3
  121.8 1.3 maximum_dynamic-update-slice_fusion.2
  123.1 1.3 maximum_dynamic-update-slice_fusion.1
  124.4 1.4 maximum_dynamic-update-slice_fusion
  125.8 1.1 pad_dynamic-update-slice_fusion.7
  126.9 1.1 pad_dynamic-update-slice_fusion.6
  128.0 1.1 pad_dynamic-update-slice_fusion.5
  131.0 1.1 pad_dynamic-update-slice_fusion.3
  132.1 1.1 pad_dynamic-update-slice_fusion.2
  134.3 1.1 pad_dynamic-update-slice_fusion
  135.4 13.5 %fusion.9 = f32[96,2048]{1,0:T(8,128)S(1)} fusion(f32[2048,2048]{1,0:T(8,128)} %pad_dynamic-update-slice_fusion, f32[16,96,128]{2,1,0:T(8,128)S(1)} %all-to-all-done), kind=kOutput, calls=%fused_computation.33 | convolution fusion | flops 4831838208 | bytes 18350080 | tf_op jit(solution)/shard_map/dot_general | solution.py:78
  148.9 19.8 %convolution_bitcast_fusion = f32[12,16,8,128]{3,2,1,0:T(8,128)S(1)} fusion(f32[96,2048]{1,0:T(8,128)S(1)} %fusion.9, f32[2048,2048]{1,0:T(8,128)} %pad_dynamic-update-slice_fusion), kind=kOutput, calls=%fused_computation | convolution fusion | flops 4831838208 | bytes 18350080 | tf_op jit(solution)/shard_map/dot_general | solution.py:81
  169.7 5.2 %all-to-all-start.1 = ((f32[96,16,128]{2,0,1:T(8,128)}), f32[96,16,128]{2,0,1:T(8,128)S(1)}, u32[]{:S(2)}, u32[]{:S(2)}) async-start(f32[96,16,128]{2,0,1:T(8,128)} %bitcast.53), calls=%async_computation.1 | async-start | bytes 1572864 | tf_op jit(solution)/shard_map/all_to_all | solution.py:88
  175.6 12.3 %all-to-all-done.1 = f32[96,16,128]{2,0,1:T(8,128)S(1)} async-done(((f32[96,16,128]{2,0,1:T(8,128)}), f32[96,16,128]{2,0,1:T(8,128)S(1)}, u32[]{:S(2)}, u32[]{:S(2)}) %all-to-all-start.1) | async-done | bytes 786464 | tf_op jit(solution)/shard_map/all_to_all | solution.py:88
  187.9 2.7 %multiply_add_fusion = (f32[24,64,128]{2,1,0:T(8,128)}, f32[24,64,128]{2,1,0:T(8,128)}) fusion(f32[24,64,128]{2,1,0:T(8,128)S(1)} %copy-done.1, f32[24,64,128]{2,1,0:T(8,128)S(1)} %copy-done, f32[]{:T(128)S(6)} %sqrt.3, f32[]{:T(128)} %bitcast.54, f32[24,64,128]{2,1,0:T(8,128)S(1)} %bitcast.72, f32[24,64,128]{2,1,0:T(8,128)S(1)} %copy-done.2, ...), kind=kLoop, calls=%fused_computation.37 | loop fusion | flops 1572864 | bytes 5505032 | tf_op jit(solution)/shard_map/add | solution.py:91
  (49 shorter events, 21.4 us)
Async XLA Ops:
  7.2 90.8 %all-gather.3.cloned.1.call-start = ((), (), s32[]{:S(2)}) async-start(), calls=%async_computation.2 | async-start | bytes 9469952 | tf_op jit(solution)/shard_map/all_gather | solution.py:43
  8.3 18.4 %collective-permute-start.2 = (f32[960,128]{1,0:T(8,128)S(1)}, f32[960,128]{1,0:T(8,128)S(1)}, u32[]{:S(2)}, u32[]{:S(2)}) collective-permute-start(f32[960,128]{1,0:T(8,128)S(1)} %slice.126), channel_id=1, source_target_pairs={{0,15},{1,14},{2,13},{3,12},{4,11},{5,10},{6,9},{7,8},{16,31},{17,... | collective-permute-start | bytes 1474568 | tf_op jit(solution)/shard_map/ppermute | solution.py:32
  29.9 8.1 %collective-permute-start = (f32[24,2,128]{2,1,0:T(2,128)S(1)}, f32[24,2,128]{2,1,0:T(2,128)S(1)}, u32[]{:S(2)}, u32[]{:S(2)}) collective-permute-start(f32[24,2,128]{2,1,0:T(2,128)S(1)} %get-tuple-element.12), channel_id=1, source_target_pairs={{0,16},{16,32},{32,48},{48,64},{64,80},{80,96},{96,112},{112,128},... | collective-permute-start | bytes 73736 | tf_op jit(solution)/shard_map/ppermute | solution.py:12
  34.8 6.4 %collective-permute-start.1 = (f32[24,2,128]{2,1,0:T(2,128)S(1)}, f32[24,2,128]{2,1,0:T(2,128)S(1)}, u32[]{:S(2)}, u32[]{:S(2)}) collective-permute-start(f32[24,2,128]{2,1,0:T(2,128)S(1)} %get-tuple-element.13), channel_id=1, source_target_pairs={{16,0},{32,16},{48,32},{64,48},{80,64},{96,80},{112,96},{128,112},... | collective-permute-start | bytes 73736 | tf_op jit(solution)/shard_map/ppermute | solution.py:13
  45.5 89.9 %all-to-all-start = ((f32[16,96,128]{2,1,0:T(8,128)}), f32[16,96,128]{2,1,0:T(8,128)S(1)}, u32[]{:S(2)}, u32[]{:S(2)}) async-start(f32[16,96,128]{2,1,0:T(8,128)} %bitcast), calls=%async_computation | async-start | bytes 1572864 | tf_op jit(solution)/shard_map/all_to_all | solution.py:77
  135.4 52.5 %copy-start = (f32[24,64,128]{2,1,0:T(8,128)S(1)}, f32[24,64,128]{2,1,0:T(8,128)}, u32[]{:S(2)}) copy-start(f32[24,64,128]{2,1,0:T(8,128)} %param.7) | copy-start | bytes 2359300
  135.4 52.5 %copy-start.1 = (f32[24,64,128]{2,1,0:T(8,128)S(1)}, f32[24,64,128]{2,1,0:T(8,128)}, u32[]{:S(2)}) copy-start(f32[24,64,128]{2,1,0:T(8,128)} %param.10) | copy-start | bytes 2359300
  135.4 52.5 %copy-start.2 = (f32[24,64,128]{2,1,0:T(8,128)S(1)}, f32[24,64,128]{2,1,0:T(8,128)}, u32[]{:S(2)}) copy-start(f32[24,64,128]{2,1,0:T(8,128)} %param.9) | copy-start | bytes 2359300
  169.7 18.2 %all-to-all-start.1 = ((f32[96,16,128]{2,0,1:T(8,128)}), f32[96,16,128]{2,0,1:T(8,128)S(1)}, u32[]{:S(2)}, u32[]{:S(2)}) async-start(f32[96,16,128]{2,0,1:T(8,128)} %bitcast.53), calls=%async_computation.1 | async-start | bytes 1572864 | tf_op jit(solution)/shard_map/all_to_all | solution.py:88
Sparse Core Ops, SparseCore 0:
  29.1 68.8 all-gather.2
where the time goes:
time: 199 us; the launch traced here: 197 us
  waiting for transfers between devices  71.3 us (36%)
  matrix products  33.3 us (17%)
  local copies, waits for them, and re-layouts  29.8 us (15%)
  starting transfers between devices  26.5 us (13%)
  other arithmetic  21.5 us (11%)
  between operations  15 us (8%)
    all_gather x1, waiting for transfers between devices, gather_factor(): gathered = lax.all_gather(piece, 'tm', axis=0, tiled=False)  44.7 us
    dot_general x1, matrix products, local(): lax.dot_general(projected, full, (((1,), (1,)), ((), ())), precision=lax....  19.8 us
    dot_general x1, matrix products, local(): jnp.dot(by_cell, full, precision=lax.Precision.HIGHEST, preferred_element...  13.5 us
    all_to_all x1, waiting for transfers between devices, local(): prior = lax.all_to_all(prior_cells, 'tm', 1, 0, tiled=True)  12.3 us
    ppermute x1, waiting for transfers between devices, gather_factor(): sent = lax.ppermute(chol_cols[T - tail:], 'tm', pairs)  11 us
    unnamed x8, other arithmetic  10.7 us
    squeeze x8, local copies, waits for them, and re-layouts, gather_factor(): nonzero = gathered[c, length_p:]  7.81 us
    all_to_all x1, starting transfers between devices, local(): by_cell = lax.all_to_all(flattened, 'tm', 0, 1, tiled=True)  7.71 us
  transfers between devices with their start and end apart: 6, of which 4 were waited for; matrix products, arithmetic and copies ran while one was open for 22% of the time, Pallas kernels for 0%

commit v1 on v0

--- a/solution.py
+++ b/solution.py
@@ -74,7 +74,10 @@
     spatial = operate(first_pass, kappa_wide[:, 1:-1])
     cell_count = row_count * col_count
     flattened = spatial.reshape(cell_count, time_count)
-    by_cell = lax.all_to_all(flattened, "tm", 0, 1, tiled=True)
+    by_cell = jnp.concatenate(
+        lax.all_to_all(jnp.stack(jnp.split(flattened, lax.axis_size("tm"), axis=0)), "tm", 0, 0),
+        axis=1,
+    )
     projected = jnp.dot(
         by_cell, full, precision=lax.Precision.HIGHEST, preferred_element_type=jnp.float32
     )

time: 199 us -> 199 us (level)
  local copies, waits for them, and re-layouts: 29.8 us -> 39.8 us
  waiting for transfers between devices: 71.3 us -> 62.1 us
    unnamed x13 -> x28, local copies, waits for them, and re-layouts: 7.64 us -> 17 us
    all_gather x1, waiting for transfers between devices: 44.7 us -> 35.6 us  [gather_factor(): gathered = lax.all_gather(piece, 'tm', axis=0, tiled=False)]
  transfers between devices with their start and end apart: 6 -> 6, of which waited for: 4 -> 4; matrix products, arithmetic and copies ran while one was open for 22% -> 27% of each run, Pallas kernels for 0% -> 0%
where the time goes in v1:
time: 199 us; the launch traced here: 197 us
  waiting for transfers between devices  62.1 us (31%)
  local copies, waits for them, and re-layouts  39.8 us (20%)
  matrix products  33.3 us (17%)
  starting transfers between devices  26.5 us (13%)
  other arithmetic  20.6 us (10%)
  between operations  15 us (8%)
    all_gather x1, waiting for transfers between devices, gather_factor(): gathered = lax.all_gather(piece, 'tm', axis=0, tiled=False)  35.6 us
    dot_general x1, matrix products, local(): lax.dot_general(projected, full, (((1,), (1,)), ((), ())), precision=lax....  19.8 us
    unnamed x28, local copies, waits for them, and re-layouts  17 us
    dot_general x1, matrix products, local(): jnp.dot(by_cell, full, precision=lax.Precision.HIGHEST, preferred_element...  13.5 us
    all_to_all x1, waiting for transfers between devices, local(): prior = lax.all_to_all(prior_cells, 'tm', 1, 0, tiled=True)  12.3 us
    ppermute x1, waiting for transfers between devices, gather_factor(): sent = lax.ppermute(chol_cols[T - tail:], 'tm', pairs)  11 us
    unnamed x8, other arithmetic  10.7 us
    squeeze x8, local copies, waits for them, and re-layouts, gather_factor(): nonzero = gathered[c, length_p:]  7.81 us
  transfers between devices with their start and end apart: 6, of which 4 were waited for; matrix products, arithmetic and copies ran while one was open for 27% of the time, Pallas kernels for 0%

profile of v1, /device:TPU:1, one launch (start us, length us, event | category | flops | bytes accessed | tf_op | source)
XLA Modules:
  0.0 197.4 jit_solution(6876970166297685279)
XLA Ops:
  8.3 7.4 %collective-permute-start.2 = (f32[960,128]{1,0:T(8,128)S(1)}, f32[960,128]{1,0:T(8,128)S(1)}, u32[]{:S(2)}, u32[]{:S(2)}) collective-permute-start(f32[960,128]{1,0:T(8,128)S(1)} %slice.126), channel_id=1, source_target_pairs={{0,15},{1,14},{2,13},{3,12},{4,11},{5,10},{6,9},{7,8},{16,31},{17,... | collective-permute-start | bytes 1474568 | tf_op jit(solution)/shard_map/ppermute | solution.py:32
  15.7 11.0 %collective-permute-done.2 = f32[960,128]{1,0:T(8,128)S(1)} collective-permute-done((f32[960,128]{1,0:T(8,128)S(1)}, f32[960,128]{1,0:T(8,128)S(1)}, u32[]{:S(2)}, u32[]{:S(2)}) %collective-permute-start.2) | collective-permute-done | bytes 491552 | tf_op jit(solution)/shard_map/ppermute | solution.py:32
  26.7 2.3 %fusion.13 = f32[1088,128]{1,0:T(8,128)} fusion(s32[]{:T(128)S(6)} %select_n.29, f32[960,128]{1,0:T(8,128)S(1)} %collective-permute-done.2, f32[2048,128]{1,0:T(8,128)} %param.12, s32[]{:T(128)S(6)} %select_n.28, pred[1088]{0:T(1024)(128)(4,1)S(1)} %iota_compare_fusion, pred[]{:T(512)S(6)} %lt.20), kind=kLoop, calls=%fused_computation.40 | loop fusion | flops 278528 | bytes 2163785 | tf_op jit(solution)/shard_map/jit(_where)/select_n | solution.py:42
  29.9 4.9 %collective-permute-start = (f32[24,2,128]{2,1,0:T(2,128)S(1)}, f32[24,2,128]{2,1,0:T(2,128)S(1)}, u32[]{:S(2)}, u32[]{:S(2)}) collective-permute-start(f32[24,2,128]{2,1,0:T(2,128)S(1)} %get-tuple-element.12), channel_id=1, source_target_pairs={{0,16},{16,32},{32,48},{48,64},{64,80},{80,96},{96,112},{112,128},... | collective-permute-start | bytes 73736 | tf_op jit(solution)/shard_map/ppermute | solution.py:12
  34.8 1.3 collective-permute-start.1
  38.0 3.3 %collective-permute-done.1 = f32[24,2,128]{2,1,0:T(2,128)S(1)} collective-permute-done((f32[24,2,128]{2,1,0:T(2,128)S(1)}, f32[24,2,128]{2,1,0:T(2,128)S(1)}, u32[]{:S(2)}, u32[]{:S(2)}) %collective-permute-start.1) | collective-permute-done | bytes 24608 | tf_op jit(solution)/shard_map/ppermute | solution.py:13
  41.3 1.2 pad_maximum_fusion
  42.5 1.7 fusion.4
  54.6 7.7 %all-to-all-start = ((f32[16,96,128]{2,1,0:T(8,128)}), f32[16,96,128]{2,1,0:T(8,128)S(1)}, u32[]{:S(2)}, u32[]{:S(2)}) async-start(f32[16,96,128]{2,1,0:T(8,128)} %constant_dynamic-update-slice_fusion), calls=%async_computation | async-start | bytes 1572864 | tf_op jit(solution)/shard_map/all_to_all | solution.py:78
  62.3 35.6 %all-gather.3.cloned.1.call-done = f32[17408,128]{1,0:T(8,128)} async-done(((f32[1088,128]{1,0:T(8,128)}), f32[17408,128]{1,0:T(8,128)}) %all-gather.3.cloned.1.call-update) | async-done | bytes 8912912 | tf_op jit(solution)/shard_map/all_gather | solution.py:43
  111.5 1.1 slice_bitcast_fusion
  112.6 2.6 %fusion.16 = (f32[1088,128]{1,0:T(8,128)S(1)}, f32[1088,128]{1,0:T(8,128)S(1)}, f32[1088,128]{1,0:T(8,128)S(1)}, f32[1088,128]{1,0:T(8,128)S(1)}, f32[1088,128]{...) fusion(f32[17408,128]{1,0:T(8,128)} %all-gather.3.cloned.1.call-done), kind=kLoop, calls=%fused_computation.95 | loop fusion | bytes 8912896 | tf_op jit(solution)/shard_map/slice | solution.py:49
  115.1 1.1 maximum_dynamic-update-slice_fusion.7
  116.2 1.4 maximum_dynamic-update-slice_fusion.6
  117.6 1.4 maximum_dynamic-update-slice_fusion.5
  119.0 1.4 maximum_dynamic-update-slice_fusion.4
  120.4 1.4 maximum_dynamic-update-slice_fusion.3
  121.8 1.3 maximum_dynamic-update-slice_fusion.2
  123.1 1.3 maximum_dynamic-update-slice_fusion.1
  124.4 1.4 maximum_dynamic-update-slice_fusion
  125.8 1.1 pad_dynamic-update-slice_fusion.7
  126.9 1.1 pad_dynamic-update-slice_fusion.6
  128.0 1.1 pad_dynamic-update-slice_fusion.5
  131.0 1.1 pad_dynamic-update-slice_fusion.3
  132.1 1.1 pad_dynamic-update-slice_fusion.2
  133.2 1.1 pad_dynamic-update-slice_fusion.1
  134.3 1.1 pad_dynamic-update-slice_fusion
  135.4 13.5 %fusion.9 = f32[96,2048]{1,0:T(8,128)S(1)} fusion(f32[2048,2048]{1,0:T(8,128)} %pad_dynamic-update-slice_fusion, f32[16,96,128]{2,1,0:T(8,128)S(1)} %all-to-all-done), kind=kOutput, calls=%fused_computation.33 | convolution fusion | flops 4831838208 | bytes 18350080 | tf_op jit(solution)/shard_map/dot_general | solution.py:81
  148.9 19.8 %convolution_bitcast_fusion = f32[12,16,8,128]{3,2,1,0:T(8,128)S(1)} fusion(f32[96,2048]{1,0:T(8,128)S(1)} %fusion.9, f32[2048,2048]{1,0:T(8,128)} %pad_dynamic-update-slice_fusion), kind=kOutput, calls=%fused_computation | convolution fusion | flops 4831838208 | bytes 18350080 | tf_op jit(solution)/shard_map/dot_general | solution.py:84
  169.7 5.2 %all-to-all-start.1 = ((f32[96,16,128]{2,0,1:T(8,128)}), f32[96,16,128]{2,0,1:T(8,128)S(1)}, u32[]{:S(2)}, u32[]{:S(2)}) async-start(f32[96,16,128]{2,0,1:T(8,128)} %bitcast.117), calls=%async_computation.1 | async-start | bytes 1572864 | tf_op jit(solution)/shard_map/all_to_all | solution.py:91
  175.6 12.3 %all-to-all-done.1 = f32[96,16,128]{2,0,1:T(8,128)S(1)} async-done(((f32[96,16,128]{2,0,1:T(8,128)}), f32[96,16,128]{2,0,1:T(8,128)S(1)}, u32[]{:S(2)}, u32[]{:S(2)}) %all-to-all-start.1) | async-done | bytes 786464 | tf_op jit(solution)/shard_map/all_to_all | solution.py:91
  187.9 2.7 %multiply_add_fusion = (f32[24,64,128]{2,1,0:T(8,128)}, f32[24,64,128]{2,1,0:T(8,128)}) fusion(f32[24,64,128]{2,1,0:T(8,128)S(1)} %copy-done.1, f32[24,64,128]{2,1,0:T(8,128)S(1)} %copy-done, f32[]{:T(128)S(6)} %sqrt.3, f32[]{:T(128)} %bitcast.118, f32[24,64,128]{2,1,0:T(8,128)S(1)} %bitcast.152, f32[24,64,128]{2,1,0:T(8,128)S(1)} %copy-done.2, ...), kind=kLoop, calls=%fused_computation.37 | loop fusion | flops 1572864 | bytes 5505032 | tf_op jit(solution)/shard_map/add | solution.py:94
  (65 shorter events, 30.6 us)
Async XLA Ops:
  7.2 90.8 %all-gather.3.cloned.1.call-start = ((), (), s32[]{:S(2)}) async-start(), calls=%async_computation.2 | async-start | bytes 9469952 | tf_op jit(solution)/shard_map/all_gather | solution.py:43
  8.3 18.4 %collective-permute-start.2 = (f32[960,128]{1,0:T(8,128)S(1)}, f32[960,128]{1,0:T(8,128)S(1)}, u32[]{:S(2)}, u32[]{:S(2)}) collective-permute-start(f32[960,128]{1,0:T(8,128)S(1)} %slice.126), channel_id=1, source_target_pairs={{0,15},{1,14},{2,13},{3,12},{4,11},{5,10},{6,9},{7,8},{16,31},{17,... | collective-permute-start | bytes 1474568 | tf_op jit(solution)/shard_map/ppermute | solution.py:32
  29.9 8.1 %collective-permute-start = (f32[24,2,128]{2,1,0:T(2,128)S(1)}, f32[24,2,128]{2,1,0:T(2,128)S(1)}, u32[]{:S(2)}, u32[]{:S(2)}) collective-permute-start(f32[24,2,128]{2,1,0:T(2,128)S(1)} %get-tuple-element.12), channel_id=1, source_target_pairs={{0,16},{16,32},{32,48},{48,64},{64,80},{80,96},{96,112},{112,128},... | collective-permute-start | bytes 73736 | tf_op jit(solution)/shard_map/ppermute | solution.py:12
  34.8 6.4 %collective-permute-start.1 = (f32[24,2,128]{2,1,0:T(2,128)S(1)}, f32[24,2,128]{2,1,0:T(2,128)S(1)}, u32[]{:S(2)}, u32[]{:S(2)}) collective-permute-start(f32[24,2,128]{2,1,0:T(2,128)S(1)} %get-tuple-element.13), channel_id=1, source_target_pairs={{16,0},{32,16},{48,32},{64,48},{80,64},{96,80},{112,96},{128,112},... | collective-permute-start | bytes 73736 | tf_op jit(solution)/shard_map/ppermute | solution.py:13
  54.6 80.8 %all-to-all-start = ((f32[16,96,128]{2,1,0:T(8,128)}), f32[16,96,128]{2,1,0:T(8,128)S(1)}, u32[]{:S(2)}, u32[]{:S(2)}) async-start(f32[16,96,128]{2,1,0:T(8,128)} %constant_dynamic-update-slice_fusion), calls=%async_computation | async-start | bytes 1572864 | tf_op jit(solution)/shard_map/all_to_all | solution.py:78
  135.4 52.5 %copy-start = (f32[24,64,128]{2,1,0:T(8,128)S(1)}, f32[24,64,128]{2,1,0:T(8,128)}, u32[]{:S(2)}) copy-start(f32[24,64,128]{2,1,0:T(8,128)} %param.7) | copy-start | bytes 2359300
  135.4 52.5 %copy-start.1 = (f32[24,64,128]{2,1,0:T(8,128)S(1)}, f32[24,64,128]{2,1,0:T(8,128)}, u32[]{:S(2)}) copy-start(f32[24,64,128]{2,1,0:T(8,128)} %param.10) | copy-start | bytes 2359300
  135.4 52.5 %copy-start.2 = (f32[24,64,128]{2,1,0:T(8,128)S(1)}, f32[24,64,128]{2,1,0:T(8,128)}, u32[]{:S(2)}) copy-start(f32[24,64,128]{2,1,0:T(8,128)} %param.9) | copy-start | bytes 2359300
  169.7 18.2 %all-to-all-start.1 = ((f32[96,16,128]{2,0,1:T(8,128)}), f32[96,16,128]{2,0,1:T(8,128)S(1)}, u32[]{:S(2)}, u32[]{:S(2)}) async-start(f32[96,16,128]{2,0,1:T(8,128)} %bitcast.117), calls=%async_computation.1 | async-start | bytes 1572864 | tf_op jit(solution)/shard_map/all_to_all | solution.py:91
Sparse Core Ops, SparseCore 0:
  29.1 68.8 all-gather.2
